TPU v7x, 32 devices: a whole 2x2x4 slice. The times are simulated.
32 devices in a mesh: grp: 2 (over y), evt: 4 (over z), var: 2 (over x), chan: 2 (over core).
Axes of the slice: x: 2, y: 2, z: 4, core: 2. Of those that a mesh axis runs over, the one named last changes fastest.
Arguments:
- variation_weights: bfloat16 [2, 32768, 1024], P('chan', ('grp', 'evt'), 'var'), parts along dimension 1, may hold values from -6 to 6
- bin_response: bfloat16 [2, 32768, 128], P('chan', ('grp', 'evt')), parts along dimension 1, may hold values from 0 to 0.25
- bin_block: int32 [2, 256], P('chan', ('grp', 'evt')), parts along dimension 1, may hold values from 0 to 127
- variation_coefficient: float32 [1024], replicated, may hold values from -4 to 4
- nuisance_index: int32 [1024], replicated, may hold values from 0 to 511, as said below
- expected: float32 [2, 32768], P('chan', ('grp', 'evt', 'var')), parts along dimension 1, may hold values from 1 to 16
- excess_counts: float32 [2, 32768], P('chan', ('grp', 'evt', 'var')), parts along dimension 1, may hold values from -10 to 10
Outputs:
- templates: float32 [2, 32768, 1024], P('chan', ('grp', 'evt', 'var')), parts along dimension 1
- nuisance_pulls: float32 [1024], P('grp'), parts along dimension 0
There are 2 independent parts, one for each index of `grp`. A program takes and returns all parts, laid end to end along the dimension named above; an argument that names none is the same for every part. Nothing has to cross between parts.
Inputs may be any that keep to these rules, and one draw needn't show every extreme that they name: `nuisance_index`: each of the 512 nuisances is named by exactly 2 variations.
All inputs are finite; a program needn't handle non-finite values.
Results may differ from a plain program's by a relative error of at most 0.0085.
Values may be sent and summed in bfloat16 or wider, within the bound.
A program may use at most 128 MiB of HBM per device.

v0:
```python
import jax
import jax.numpy as jnp
from jax import lax
from jax.sharding import PartitionSpec as P

BLK = 128
CH_BINS = 16384
NUIS = 512


def shards(
    variation_weights,
    bin_response,
    bin_block,
    variation_coefficient,
    nuisance_index,
    expected,
    excess_counts,
):
    weights = variation_weights[0]
    response = bin_response[0]
    blocks = bin_block[0]
    evt_count = lax.axis_size("evt")
    nblocks = blocks.shape[0]
    var_local = weights.shape[1]
    products = jnp.einsum(
        "ket,kev->ktv",
        response.reshape(nblocks, BLK, BLK),
        weights.reshape(nblocks, BLK, var_local),
        preferred_element_type=jnp.float32,
    )
    targets = lax.iota(jnp.int32, CH_BINS // evt_count * lax.axis_size("evt") // BLK)
    select = (blocks[None, :] == targets[:, None]).astype(jnp.float32)
    block_term = jnp.einsum("qk,ktv->qtv", select, products, precision=lax.Precision.HIGHEST)
    summed = lax.psum_scatter(
        block_term.reshape(CH_BINS // evt_count * lax.axis_size("evt"), var_local).astype(
            jnp.bfloat16
        ),
        "evt",
        scatter_dimension=0,
        tiled=True,
    ).astype(jnp.float32)
    local_templates = lax.all_to_all(
        summed.astype(jnp.bfloat16), "var", split_axis=0, concat_axis=1, tiled=True
    ).astype(summed.dtype)
    mixing = (nuisance_index[:, None] == lax.iota(jnp.int32, NUIS)[None, :]).astype(
        jnp.float32
    ) * variation_coefficient[:, None]
    jacobian = jnp.dot(local_templates, mixing, precision=lax.Precision.HIGHEST)
    inverse = 1.0 / expected[0]
    scaled = jacobian * inverse[:, None]
    gram_matrix = lax.dot_general(
        scaled, jacobian, (((0,), (0,)), ((), ())), precision=lax.Precision.HIGHEST
    )
    gradient = jnp.dot(excess_counts[0] * inverse, jacobian, precision=lax.Precision.HIGHEST)
    gram_matrix, gradient = lax.psum((gram_matrix, gradient), ("evt", "var", "chan"))
    gram_matrix = gram_matrix + jnp.eye(NUIS, dtype=jnp.float32)
    factor = jnp.linalg.cholesky(gram_matrix)
    step_sizes = jax.scipy.linalg.cho_solve((factor, True), gradient)
    nuisance_pulls = step_sizes * jnp.sqrt(jnp.diagonal(gram_matrix))
    return (local_templates[None], nuisance_pulls)


def solution(mesh):
    placed = (
        P("chan", ("grp", "evt"), "var"),
        P("chan", ("grp", "evt"), None),
        P("chan", ("grp", "evt")),
        P(),
        P(),
        P("chan", ("grp", "evt", "var")),
        P("chan", ("grp", "evt", "var")),
    )
    return jax.shard_map(
        shards,
        mesh=mesh,
        in_specs=placed,
        out_specs=(P("chan", ("grp", "evt", "var"), None), P("grp")),
        check_vma=False,
    )
```

profile of v0, /device:TPU:0, one launch (start us, length us, event | category | flops | bytes accessed | tf_op | source)
XLA Modules:
  0.0 670.6 jit_solution(15033247227140351277)
XLA Ops:
  11.9 17.4 %convolution_convert_fusion = bf16[128,128,512]{2,0,1:T(8,128)(2,1)} fusion(f32[32,128,512]{2,1,0:T(8,128)S(1)} %fusion.70, s32[32]{0:T(128)S(1)} %bitcast.179), kind=kOutput, calls=%fused_computation.3 | convolution fusion | flops 3229618176 | bytes 25165952 | tf_op jit(solution)/shard_map/qk,ktv->qtv/dot_general | solution.py:34
  29.3 18.5 %copy.16 = bf16[128,128,512]{2,1,0:T(8,128)(2,1)} copy(bf16[128,128,512]{2,0,1:T(8,128)(2,1)} %convolution_convert_fusion) | data formatting | bytes 33554432 | tf_op jit(solution)/shard_map/convert_element_type | solution.py:36
  47.8 283.1 %reduce-scatter.2.cloned.1.call-done = bf16[4096,512]{1,0:T(8,128)(2,1)} async-done(((bf16[16384,512]{1,0:T(8,128)(2,1)}), bf16[4096,512]{1,0:T(8,128)(2,1)}) %reduce-scatter.2.cloned.1.call-update) | async-done | bytes 4194320 | tf_op jit(solution)/shard_map/reduce_scatter | solution.py:35
  331.0 5.7 all-to-all-start
  336.9 47.4 %all-to-all-done = bf16[2,2048,512]{2,1,0:T(8,128)(2,1)} async-done(((bf16[2,2048,512]{2,1,0:T(8,128)(2,1)}), bf16[2,2048,512]{2,1,0:T(8,128)(2,1)}, u32[]{:S(2)}, u32[]{:S(2)}) %all-to-all-start) | async-done | bytes 4194336 | tf_op jit(solution)/shard_map/all_to_all | solution.py:43
  384.2 6.2 copy.18
  390.5 9.6 %fusion.4 = f32[2048,512]{1,0:T(8,128)S(1)} fusion(bf16[2048,1024]{0,1:T(8,128)(2,1)} %bitcast.167, f32[1024]{0:T(1024)S(1)} %copy-done.8, s32[1024]{0:T(1024)S(1)} %copy-done.9), kind=kOutput, calls=%fused_computation.8 | convolution fusion | flops 12885950464 | bytes 8396800 | tf_op jit(solution)/shard_map/dot_general | solution.py:49
  402.1 9.0 %fusion.1 = f32[512,512]{0,1:T(8,128)} fusion(f32[2048,512]{1,0:T(8,128)S(1)} %fusion.4, f32[2048]{0:T(1024)S(1)} %bitcast.169), kind=kOutput, calls=%fused_computation.5 | convolution fusion | flops 6443499520 | bytes 5251072 | tf_op jit(solution)/shard_map/dot_general | solution.py:52
  411.1 6.8 %bitcast_convert_fusion = f32[2048,2,512]{2,0,1:T(8,128)} fusion(bf16[2,2048,512]{2,1,0:T(8,128)(2,1)} %all-to-all-done), kind=kLoop, calls=%fused_computation.120 | loop fusion | flops 2097152 | bytes 12582912 | tf_op jit(solution)/shard_map/convert_element_type | solution.py:45
  417.9 8.7 %copy.17 = f32[2048,2,512]{0,2,1:T(8,128)} copy(f32[2048,2,512]{2,0,1:T(8,128)} %bitcast_convert_fusion) | data formatting | bytes 16777216 | tf_op jit(solution)/shard_map/convert_element_type | solution.py:45
  426.6 9.3 %copy.21 = f32[1,2048,1024]{2,1,0:T(8,128)} copy(f32[1,2048,1024]{1,2,0:T(8,128)} %bitcast.164) | data formatting | bytes 16777216
  435.9 4.3 fusion.71
  440.2 32.0 %psum.15 = f32[512]{0:T(512)S(1)} all-reduce(f32[512]{0:T(512)S(1)} %bitcast.175), channel_id=1, replica_groups=mesh['grp'=2,'evt'=4,'var'=2,'chan'=2] {'evt','var','chan'}, use_global_device_ids=true, to_apply=%region_10.11 | all-reduce | flops 512 | bytes 4096 | tf_op jit(solution)/shard_map/psum | solution.py:56
  472.2 32.2 %all-reduce.3.cloned.1.call-done = f32[512,512]{0,1:T(8,128)} async-done(((f32[512,512]{0,1:T(8,128)}), f32[512,512]{0,1:T(8,128)}) %all-reduce.3.cloned.1.call-update) | async-done | bytes 1048592 | tf_op jit(solution)/shard_map/psum | solution.py:56
  507.4 11.7 %cholesky.104 = f32[128,128]{1,0:T(8,128)S(1)} custom-call(f32[128,128]{1,0:T(8,128)S(1)} %cholesky.266), custom_call_target="Cholesky" | custom-call | tf_op jit(solution)/shard_map/jit(cholesky)/cholesky | solution.py:58
  519.2 9.8 %custom-call.34 = f32[1,128,128]{1,2,0:T(8,128)S(1)} custom-call(f32[1,128,128]{2,1,0:T(8,128)S(1)} %get-tuple-element.31), custom_call_target="InvertDiagBlocksLowerTriangular" | custom-call | tf_op jit(solution)/shard_map/jit(cholesky)/cholesky | solution.py:58
  531.6 11.7 %cholesky.217 = f32[128,128]{1,0:T(8,128)S(1)} custom-call(f32[128,128]{1,0:T(8,128)S(1)} %cholesky.270), custom_call_target="Cholesky" | custom-call | tf_op jit(solution)/shard_map/jit(cholesky)/cholesky | solution.py:58
  543.4 10.2 %custom-call.35 = f32[1,128,128]{1,2,0:T(8,128)S(1)} custom-call(f32[1,128,128]{2,1,0:T(8,128)S(1)} %get-tuple-element.28), custom_call_target="InvertDiagBlocksLowerTriangular" | custom-call | tf_op jit(solution)/shard_map/jit(cholesky)/cholesky | solution.py:58
  555.2 11.7 %cholesky.238 = f32[128,128]{1,0:T(8,128)S(1)} custom-call(f32[128,128]{1,0:T(8,128)S(1)} %cholesky.275), custom_call_target="Cholesky" | custom-call | tf_op jit(solution)/shard_map/jit(cholesky)/cholesky | solution.py:58
  567.7 9.8 %custom-call.36 = f32[1,128,128]{1,2,0:T(8,128)S(1)} custom-call(f32[1,128,128]{2,1,0:T(8,128)S(1)} %get-tuple-element.25), custom_call_target="InvertDiagBlocksLowerTriangular" | custom-call | tf_op jit(solution)/shard_map/jit(cholesky)/cholesky | solution.py:58
  578.9 11.7 %cholesky.255 = f32[128,128]{1,0:T(8,128)S(1)} custom-call(f32[128,128]{1,0:T(8,128)S(1)} %convolution_subtract_fusion.2), custom_call_target="Cholesky" | custom-call | tf_op jit(solution)/shard_map/jit(cholesky)/cholesky | solution.py:58
  595.9 14.1 %while.1 = (s32[]{:T(128)}, f32[512,512]{1,0:T(8,128)}, s32[4,2]{0,1:T(2,128)S(1)}, f32[4,128,128]{2,1,0:T(8,128)}, s32[]{:T(128)}) while((s32[]{:T(128)}, f32[512,512]{1,0:T(8,128)}, s32[4,2]{0,1:T(2,128)S(1)}, f32[4,128,128]{2,1,0:T(8,128)}, s32[]{:T(128)}) %tuple.32), condition=%wide.while_cond, body=%wide.while_body.sunk | while | flops 2 | bytes 132705 | solution.py:59
  610.0 40.1 %custom-call.37 = f32[4,128,128]{1,2,0:T(8,128)S(1)} custom-call(f32[4,128,128]{2,1,0:T(8,128)} %get-tuple-element.9), custom_call_target="InvertDiagBlocksLowerTriangular" | custom-call | tf_op jit(solution)/shard_map/jit(_cho_solve)/triangular_solve | solution.py:59
  658.5 4.6 gather_fusion
  (80 shorter events, 41.7 us)
Async XLA Ops:
  7.2 1.2 copy-start
  7.2 323.8 %reduce-scatter.2.cloned.1.call-start = ((), (), s32[]{:S(2)}) async-start(), calls=%async_computation.2 | async-start | bytes 20971520 | tf_op jit(solution)/shard_map/reduce_scatter | solution.py:35
  8.4 3.5 copy-start.7
  331.0 5.8 copy-start.6
  331.0 5.9 copy-start.5
  331.0 53.3 %all-to-all-start = ((bf16[2,2048,512]{2,1,0:T(8,128)(2,1)}), bf16[2,2048,512]{2,1,0:T(8,128)(2,1)}, u32[]{:S(2)}, u32[]{:S(2)}) async-start(bf16[2,2048,512]{2,1,0:T(8,128)(2,1)} %bitcast.166), calls=%async_computation.1 | async-start | bytes 8388608 | tf_op jit(solution)/shard_map/all_to_all | solution.py:43
  336.7 167.7 %all-reduce.3.cloned.1.call-start = ((), (), s32[]{:S(2)}) async-start(), calls=%async_computation.3 | async-start | bytes 2097152 | tf_op jit(solution)/shard_map/psum | solution.py:56
  384.2 6.2 copy-start.8
  384.2 6.2 copy-start.9
  400.1 2.0 copy-start.2
  504.4 1.8 copy-start.3
  506.4 1.0 copy-start.4
  553.6 110.0 %copy-start.1 = (bf16[1,4096,128]{2,1,0:T(8,128)(2,1)S(1)}, bf16[1,4096,128]{2,1,0:T(8,128)(2,1)}, u32[]{:S(2)}) copy-start(bf16[1,4096,128]{2,1,0:T(8,128)(2,1)} %param.8) | copy-start | bytes 3145732
Sparse Core Ops, SparseCore 0:
  48.0 282.9 reduce-scatter.1
  411.2 93.1 all-reduce.2
where the time goes:
time: 680 us; the launch traced here: 671 us
  waiting for transfers between devices  363 us (53%)
  other arithmetic  129 us (19%)
  local copies, waits for them, and re-layouts  66.1 us (10%)
  matrix products  57.5 us (8%)
  blocking collectives  32 us (5%)
  between operations  17.3 us (3%)
    reduce_scatter x1, waiting for transfers between devices, shards(): lax.psum_scatter(block_term.reshape(CH_BINS // evt_count * lax.axis_size(...  283 us
    another operation x14, other arithmetic, shards(): factor = jnp.linalg.cholesky(gram_matrix)  78.9 us
    all_to_all x1, waiting for transfers between devices, shards(): lax.all_to_all(summed.astype(jnp.bfloat16), 'var', split_axis=0, concat_a...  47.4 us
    another operation x4, other arithmetic, shards(): step_sizes = jax.scipy.linalg.cho_solve((factor, True), gradient)  41.3 us
    psum x1, waiting for transfers between devices, shards(): lax.psum((gram_matrix, gradient), ('evt', 'var', 'chan'))  32.2 us
    psum x1, blocking collectives, shards(): lax.psum((gram_matrix, gradient), ('evt', 'var', 'chan'))  32 us
    convert_element_type x1, local copies, waits for them, and re-layouts, shards(): block_term.reshape(CH_BINS // evt_count * lax.axis_size('evt'), var_local)  18.5 us
    dot_general x1, matrix products, shards(): jnp.einsum('qk,ktv->qtv', select, products, precision=lax.Precision.HIGHEST)  17.4 us
  transfers between devices with their start and end apart: 3, of which 3 were waited for; matrix products, arithmetic and copies ran while one was open for 4% of the time, Pallas kernels for 0%

commit v1 on v0

--- a/solution.py
+++ b/solution.py
@@ -53,7 +53,7 @@
         scaled, jacobian, (((0,), (0,)), ((), ())), precision=lax.Precision.HIGHEST
     )
     gradient = jnp.dot(excess_counts[0] * inverse, jacobian, precision=lax.Precision.HIGHEST)
-    gram_matrix, gradient = lax.psum((gram_matrix, gradient), ("evt", "var", "chan"))
+    gram_matrix, gradient = lax.psum(lax.psum((gram_matrix, gradient), ("var", "chan")), "evt")
     gram_matrix = gram_matrix + jnp.eye(NUIS, dtype=jnp.float32)
     factor = jnp.linalg.cholesky(gram_matrix)
     step_sizes = jax.scipy.linalg.cho_solve((factor, True), gradient)

time: 680 us -> 678 us (level)
  blocking collectives: 32 us -> 17.9 us
  waiting for transfers between devices: 363 us -> 375 us
    psum x1 -> x2, blocking collectives: 32 us -> 17.9 us  [the longest x1 12.1 us: shards(): lax.psum(lax.psum((gram_matrix, gradient), ('var', 'chan')), 'evt')]
    psum x1 -> x2, waiting for transfers between devices: 32.2 us -> 44 us  [the longest x1 36.2 us: shards(): lax.psum((gram_matrix, gradient), ('var', 'chan'))]
  transfers between devices with their start and end apart: 3 -> 4, of which waited for: 3 -> 4; matrix products, arithmetic and copies ran while one was open for 4% -> 4% of each run, Pallas kernels for 0% -> 0%
where the time goes in v1:
time: 678 us; the launch traced here: 668 us
  waiting for transfers between devices  375 us (55%)
  other arithmetic  129 us (19%)
  local copies, waits for them, and re-layouts  66.1 us (10%)
  matrix products  57.5 us (8%)
  blocking collectives  17.9 us (3%)
  between operations  17 us (3%)
    reduce_scatter x1, waiting for transfers between devices, shards(): lax.psum_scatter(block_term.reshape(CH_BINS // evt_count * lax.axis_size(...  283 us
    another operation x14, other arithmetic, shards(): factor = jnp.linalg.cholesky(gram_matrix)  78.9 us
    all_to_all x1, waiting for transfers between devices, shards(): lax.all_to_all(summed.astype(jnp.bfloat16), 'var', split_axis=0, concat_a...  47.4 us
    another operation x4, other arithmetic, shards(): step_sizes = jax.scipy.linalg.cho_solve((factor, True), gradient)  41.3 us
    psum x1, waiting for transfers between devices, shards(): lax.psum((gram_matrix, gradient), ('var', 'chan'))  36.2 us
    convert_element_type x1, local copies, waits for them, and re-layouts, shards(): block_term.reshape(CH_BINS // evt_count * lax.axis_size('evt'), var_local)  18.5 us
    dot_general x1, matrix products, shards(): jnp.einsum('qk,ktv->qtv', select, products, precision=lax.Precision.HIGHEST)  17.4 us
    another operation x12, local copies, waits for them, and re-layouts  14.1 us
  transfers between devices with their start and end apart: 4, of which 4 were waited for; matrix products, arithmetic and copies ran while one was open for 4% of the time, Pallas kernels for 0%

profile of v1, /device:TPU:0, one launch (start us, length us, event | category | flops | bytes accessed | tf_op | source)
XLA Modules:
  0.0 668.2 jit_solution(17557415232742538163)
XLA Ops:
  11.9 17.4 %convolution_convert_fusion = bf16[128,128,512]{2,0,1:T(8,128)(2,1)} fusion(f32[32,128,512]{2,1,0:T(8,128)S(1)} %fusion.70, s32[32]{0:T(128)S(1)} %bitcast.179), kind=kOutput, calls=%fused_computation.3 | convolution fusion | flops 3229618176 | bytes 25165952 | tf_op jit(solution)/shard_map/qk,ktv->qtv/dot_general | solution.py:34
  29.3 18.5 %copy.16 = bf16[128,128,512]{2,1,0:T(8,128)(2,1)} copy(bf16[128,128,512]{2,0,1:T(8,128)(2,1)} %convolution_convert_fusion) | data formatting | bytes 33554432 | tf_op jit(solution)/shard_map/convert_element_type | solution.py:36
  47.8 283.2 %reduce-scatter.2.cloned.1.call-done = bf16[4096,512]{1,0:T(8,128)(2,1)} async-done(((bf16[16384,512]{1,0:T(8,128)(2,1)}), bf16[4096,512]{1,0:T(8,128)(2,1)}) %reduce-scatter.2.cloned.1.call-update) | async-done | bytes 4194320 | tf_op jit(solution)/shard_map/reduce_scatter | solution.py:35
  331.0 5.7 all-to-all-start
  336.8 47.4 %all-to-all-done = bf16[2,2048,512]{2,1,0:T(8,128)(2,1)} async-done(((bf16[2,2048,512]{2,1,0:T(8,128)(2,1)}), bf16[2,2048,512]{2,1,0:T(8,128)(2,1)}, u32[]{:S(2)}, u32[]{:S(2)}) %all-to-all-start) | async-done | bytes 4194336 | tf_op jit(solution)/shard_map/all_to_all | solution.py:43
  384.2 6.2 copy.18
  390.5 9.6 %fusion.4 = f32[2048,512]{1,0:T(8,128)S(1)} fusion(bf16[2048,1024]{0,1:T(8,128)(2,1)} %bitcast.167, f32[1024]{0:T(1024)S(1)} %copy-done.8, s32[1024]{0:T(1024)S(1)} %copy-done.9), kind=kOutput, calls=%fused_computation.8 | convolution fusion | flops 12885950464 | bytes 8396800 | tf_op jit(solution)/shard_map/dot_general | solution.py:49
  402.1 9.0 %fusion.1 = f32[512,512]{0,1:T(8,128)} fusion(f32[2048,512]{1,0:T(8,128)S(1)} %fusion.4, f32[2048]{0:T(1024)S(1)} %bitcast.168), kind=kOutput, calls=%fused_computation.5 | convolution fusion | flops 6443499520 | bytes 5251072 | tf_op jit(solution)/shard_map/dot_general | solution.py:52
  411.2 36.2 %all-reduce.4.cloned.1.call-done = f32[512,512]{0,1:T(8,128)} async-done(((f32[512,512]{0,1:T(8,128)}), f32[512,512]{0,1:T(8,128)}) %all-reduce.4.cloned.1.call-update) | async-done | bytes 1048592 | tf_op jit(solution)/shard_map/psum | solution.py:56
  447.4 6.8 %bitcast_convert_fusion = f32[2048,2,512]{2,0,1:T(8,128)} fusion(bf16[2,2048,512]{2,1,0:T(8,128)(2,1)} %all-to-all-done), kind=kLoop, calls=%fused_computation.120 | loop fusion | flops 2097152 | bytes 12582912 | tf_op jit(solution)/shard_map/convert_element_type | solution.py:45
  454.2 8.8 %copy.17 = f32[2048,2,512]{0,2,1:T(8,128)} copy(f32[2048,2,512]{2,0,1:T(8,128)} %bitcast_convert_fusion) | data formatting | bytes 16777216 | tf_op jit(solution)/shard_map/convert_element_type | solution.py:45
  462.9 9.3 %copy.21 = f32[1,2048,1024]{2,1,0:T(8,128)} copy(f32[1,2048,1024]{1,2,0:T(8,128)} %bitcast.164) | data formatting | bytes 16777216
  476.5 5.9 psum.30
  482.4 12.1 %psum.31 = f32[512]{0:T(512)S(1)} all-reduce(f32[512]{0:T(512)S(1)} %psum.30), channel_id=1, replica_groups=mesh['grp'=2,'evt'=4,'var'=2,'chan'=2] {'evt'}, use_global_device_ids=true, to_apply=%region_12.13 | all-reduce | flops 512 | bytes 4096 | tf_op jit(solution)/shard_map/psum | solution.py:56
  494.4 7.8 %all-reduce.6.cloned.1.call-done = f32[512,512]{0,1:T(8,128)} async-done(((f32[512,512]{0,1:T(8,128)}), f32[512,512]{0,1:T(8,128)}) %all-reduce.6.cloned.1.call-update) | async-done | bytes 1048592 | tf_op jit(solution)/shard_map/psum | solution.py:56
  505.3 11.7 %cholesky.104 = f32[128,128]{1,0:T(8,128)S(1)} custom-call(f32[128,128]{1,0:T(8,128)S(1)} %cholesky.266), custom_call_target="Cholesky" | custom-call | tf_op jit(solution)/shard_map/jit(cholesky)/cholesky | solution.py:58
  517.0 9.8 %custom-call.34 = f32[1,128,128]{1,2,0:T(8,128)S(1)} custom-call(f32[1,128,128]{2,1,0:T(8,128)S(1)} %get-tuple-element.31), custom_call_target="InvertDiagBlocksLowerTriangular" | custom-call | tf_op jit(solution)/shard_map/jit(cholesky)/cholesky | solution.py:58
  529.5 11.7 %cholesky.217 = f32[128,128]{1,0:T(8,128)S(1)} custom-call(f32[128,128]{1,0:T(8,128)S(1)} %cholesky.270), custom_call_target="Cholesky" | custom-call | tf_op jit(solution)/shard_map/jit(cholesky)/cholesky | solution.py:58
  541.2 10.2 %custom-call.35 = f32[1,128,128]{1,2,0:T(8,128)S(1)} custom-call(f32[1,128,128]{2,1,0:T(8,128)S(1)} %get-tuple-element.28), custom_call_target="InvertDiagBlocksLowerTriangular" | custom-call | tf_op jit(solution)/shard_map/jit(cholesky)/cholesky | solution.py:58
  553.0 11.7 %cholesky.238 = f32[128,128]{1,0:T(8,128)S(1)} custom-call(f32[128,128]{1,0:T(8,128)S(1)} %cholesky.275), custom_call_target="Cholesky" | custom-call | tf_op jit(solution)/shard_map/jit(cholesky)/cholesky | solution.py:58
  565.5 9.8 %custom-call.36 = f32[1,128,128]{1,2,0:T(8,128)S(1)} custom-call(f32[1,128,128]{2,1,0:T(8,128)S(1)} %get-tuple-element.25), custom_call_target="InvertDiagBlocksLowerTriangular" | custom-call | tf_op jit(solution)/shard_map/jit(cholesky)/cholesky | solution.py:58
  576.8 11.7 %cholesky.255 = f32[128,128]{1,0:T(8,128)S(1)} custom-call(f32[128,128]{1,0:T(8,128)S(1)} %convolution_subtract_fusion.2), custom_call_target="Cholesky" | custom-call | tf_op jit(solution)/shard_map/jit(cholesky)/cholesky | solution.py:58
  593.8 14.1 %while.1 = (s32[]{:T(128)}, f32[512,512]{1,0:T(8,128)}, s32[4,2]{0,1:T(2,128)S(1)}, f32[4,128,128]{2,1,0:T(8,128)}, s32[]{:T(128)}) while((s32[]{:T(128)}, f32[512,512]{1,0:T(8,128)}, s32[4,2]{0,1:T(2,128)S(1)}, f32[4,128,128]{2,1,0:T(8,128)}, s32[]{:T(128)}) %tuple.32), condition=%wide.while_cond, body=%wide.while_body.sunk | while | flops 2 | bytes 132705 | solution.py:59
  607.9 40.1 %custom-call.37 = f32[4,128,128]{1,2,0:T(8,128)S(1)} custom-call(f32[4,128,128]{2,1,0:T(8,128)} %get-tuple-element.9), custom_call_target="InvertDiagBlocksLowerTriangular" | custom-call | tf_op jit(solution)/shard_map/jit(_cho_solve)/triangular_solve | solution.py:59
  (84 shorter events, 50.7 us)
Async XLA Ops:
  7.2 1.2 copy-start
  7.2 323.8 %reduce-scatter.2.cloned.1.call-start = ((), (), s32[]{:S(2)}) async-start(), calls=%async_computation.2 | async-start | bytes 20971520 | tf_op jit(solution)/shard_map/reduce_scatter | solution.py:35
  8.4 3.5 copy-start.7
  331.0 5.8 copy-start.6
  331.0 53.2 %all-to-all-start = ((bf16[2,2048,512]{2,1,0:T(8,128)(2,1)}), bf16[2,2048,512]{2,1,0:T(8,128)(2,1)}, u32[]{:S(2)}, u32[]{:S(2)}) async-start(bf16[2,2048,512]{2,1,0:T(8,128)(2,1)} %bitcast.166), calls=%async_computation.1 | async-start | bytes 8388608 | tf_op jit(solution)/shard_map/all_to_all | solution.py:43
  336.8 110.6 %all-reduce.4.cloned.1.call-start = ((), (), s32[]{:S(2)}) async-start(), calls=%async_computation.3 | async-start | bytes 2097152 | tf_op jit(solution)/shard_map/psum | solution.py:56
  384.2 6.2 copy-start.8
  384.2 6.2 copy-start.9
  400.1 2.0 copy-start.2
  402.1 9.1 %copy-start.5 = (f32[1,2048]{1,0:T(1,128)S(1)}, f32[1,2048]{1,0:T(1,128)}, u32[]{:S(2)}) copy-start(f32[1,2048]{1,0:T(1,128)} %param.13) | copy-start | bytes 24580
  411.1 91.2 %all-reduce.6.cloned.1.call-start = ((), (), s32[]{:S(2)}) async-start(), calls=%async_computation.4 | async-start | bytes 2097152 | tf_op jit(solution)/shard_map/psum | solution.py:56
  502.2 1.8 copy-start.3
  504.2 1.0 copy-start.4
  551.4 110.0 %copy-start.1 = (bf16[1,4096,128]{2,1,0:T(8,128)(2,1)S(1)}, bf16[1,4096,128]{2,1,0:T(8,128)(2,1)}, u32[]{:S(2)}) copy-start(bf16[1,4096,128]{2,1,0:T(8,128)(2,1)} %param.8) | copy-start | bytes 3145732
Sparse Core Ops, SparseCore 0:
  48.0 283.0 reduce-scatter.1
  411.2 36.1 all-reduce.3
  449.7 52.4 all-reduce.5
